TPU v7x, 32 devices: a whole 2x2x4 slice. The times are simulated.
32 devices in a mesh: dp: 8 (over z, x), mp: 4 (over y, core).
Axes of the slice: x: 2, y: 2, z: 4, core: 2. Of those that a mesh axis runs over, the one named last changes fastest.
Arguments:
- tokens: bfloat16 [32768, 768], P('dp'), may hold values from -6 to 6
- segment: int32 [32768], P('dp'), may hold values from 0 to 8, as said below
- ln1_gain: bfloat16 [768], P('mp'), may hold values from 0.5 to 1.5
- ln1_bias: bfloat16 [768], P('mp'), may hold values from -2 to 2
- w_qkv: bfloat16 [3, 768, 768], P(None, None, 'mp'), may hold values from -0.21875 to 0.21875
- b_qv: bfloat16 [2, 768], P(None, 'mp'), may hold values from -2 to 2
- w_out: bfloat16 [768, 768], P('mp'), may hold values from -0.875 to 0.875
- b_out: bfloat16 [768], P('mp'), may hold values from -2 to 2
- ln2_gain: bfloat16 [768], P('mp'), may hold values from 0.5 to 1.5
- ln2_bias: bfloat16 [768], P('mp'), may hold values from -2 to 2
- w_up: bfloat16 [768, 3072], P(None, 'mp'), may hold values from -0.21875 to 0.21875
- b_up: bfloat16 [3072], P('mp'), may hold values from -3 to 3
- w_down: bfloat16 [3072, 768], P('mp'), may hold values from -0.109375 to 0.109375
- b_down: bfloat16 [768], P('mp'), may hold values from -2 to 2
- cotangent: bfloat16 [32768, 768], P(('dp', 'mp')), may hold values from -6 to 6
Outputs:
- output: bfloat16 [32768, 768], P(('dp', 'mp'))
- grad_x: float32 [32768, 768], P(('dp', 'mp'))
- grad_ln1_gain: float32 [768], P('mp')
- grad_ln1_bias: float32 [768], P('mp')
- grad_w_qkv: float32 [3, 768, 768], P(None, None, 'mp')
- grad_b_qv: float32 [2, 768], P(None, 'mp')
- grad_w_out: float32 [768, 768], P('mp')
- grad_b_out: float32 [768], P('mp')
- grad_ln2_gain: float32 [768], P('mp')
- grad_ln2_bias: float32 [768], P('mp')
- grad_w_up: float32 [768, 3072], P(None, 'mp')
- grad_b_up: float32 [3072], P('mp')
- grad_w_down: float32 [3072, 768], P('mp')
- grad_b_down: float32 [768], P('mp')
Inputs may be any that keep to these rules, and one draw needn't show every extreme that they name: `segment`: within each aligned sequence of 512 rows the numbers never fall except to 0; 0 marks padding rows, which stand at the end of a sequence.
All inputs are finite; a program needn't handle non-finite values.
Results may differ from a plain program's by a relative error of at most 0.018.
Values may be sent and summed in bfloat16 or wider, within the bound.
A program may use at most 256 MiB of HBM per device.

v0:
```python
import jax
import jax.numpy as jnp
from jax import lax
from jax.sharding import PartitionSpec as P

HD = 64
LEN = 512


def layer_norm(values, norm_gain, norm_shift):
    centered = values - jnp.mean(values, axis=-1, keepdims=True)
    spread = jnp.mean(centered * centered, axis=-1, keepdims=True)
    return centered * lax.rsqrt(spread + 1e-06) * norm_gain + norm_shift


def norm_back(values, norm_gain, norm_shift, incoming):
    result, pull_back = jax.vjp(layer_norm, values, norm_gain, norm_shift)
    return pull_back(incoming)


def gelu_exact(values):
    return jax.nn.gelu(values, approximate=False)


def gelu_back(values, incoming):
    result, pull_back = jax.vjp(gelu_exact, values)
    return pull_back(incoming)[0]


def plain_dot(left, right):
    return jnp.dot(left, right, preferred_element_type=jnp.float32)


def over_rows(left, right):
    return lax.dot_general(
        left, right, (((0,), (0,)), ((), ())), preferred_element_type=jnp.float32
    )


def against(left, right):
    return lax.dot_general(
        left, right, (((1,), (1,)), ((), ())), preferred_element_type=jnp.float32
    )


def allowed_pairs(segment):
    length = segment.shape[0]
    row_ids = lax.broadcasted_iota(jnp.int32, (length, length), 0)
    col_ids = lax.broadcasted_iota(jnp.int32, (length, length), 1)
    same = (segment[:, None] == segment[None, :]) & (segment[None, :] != 0)
    return same | (row_ids == col_ids)


def head_scores(query_heads, key_heads, segment):
    score_scale = query_heads.shape[-1] ** (-0.5)
    scores = (
        jnp.einsum("qhd,khd->hqk", query_heads, key_heads, preferred_element_type=jnp.float32)
        * score_scale
    )
    return jnp.where(allowed_pairs(segment)[None], scores, -1e30)


def attend_forward(entries):
    query_heads, key_heads, value_heads, segment = entries
    masked = head_scores(query_heads, key_heads, segment)
    row_max = jnp.max(masked, axis=-1, keepdims=True)
    expo_scores = jnp.exp(masked - row_max)
    row_sum = jnp.sum(expo_scores, axis=-1, keepdims=True)
    attn_probs = (expo_scores / row_sum).astype(jnp.bfloat16)
    attended = jnp.einsum(
        "hqk,khd->qhd", attn_probs, value_heads, preferred_element_type=jnp.float32
    )
    return (attended.astype(jnp.bfloat16), (row_max + jnp.log(row_sum))[..., 0])


def attend_backward(entries):
    query_heads, key_heads, value_heads, segment, log_total, grad_heads = entries
    score_scale = query_heads.shape[-1] ** (-0.5)
    attn_probs = jnp.exp(head_scores(query_heads, key_heads, segment) - log_total[..., None])
    grad_probs = jnp.einsum(
        "qhd,khd->hqk", grad_heads, value_heads, preferred_element_type=jnp.float32
    )
    inner = jnp.sum(attn_probs * grad_probs, axis=-1, keepdims=True)
    grad_scores = (attn_probs * (grad_probs - inner)).astype(jnp.bfloat16)
    grad_query = (
        jnp.einsum("hqk,khd->qhd", grad_scores, key_heads, preferred_element_type=jnp.float32)
        * score_scale
    )
    grad_key = (
        jnp.einsum("hqk,qhd->khd", grad_scores, query_heads, preferred_element_type=jnp.float32)
        * score_scale
    )
    grad_value = jnp.einsum(
        "hqk,qhd->khd",
        attn_probs.astype(jnp.bfloat16),
        grad_heads,
        preferred_element_type=jnp.float32,
    )
    return (
        grad_query.astype(jnp.bfloat16),
        grad_key.astype(jnp.bfloat16),
        grad_value.astype(jnp.bfloat16),
    )


def per_device(
    tokens,
    segment,
    ln1_gain,
    ln1_bias,
    w_qkv,
    b_qv,
    w_out,
    b_out,
    ln2_gain,
    ln2_bias,
    w_up,
    b_up,
    w_down,
    b_down,
    cotangent,
):
    group_rows = tokens.shape[0]
    group_size = lax.axis_size("mp")
    my_index = lax.axis_index("mp")
    row_count = group_rows // group_size
    sequences = group_rows // LEN
    heads_here = w_qkv.shape[2] // HD
    (
        gain_one,
        shift_one,
        gain_two,
        shift_two,
        bias_out,
        bias_down,
        bias_up,
        full_out,
        full_up,
        full_down,
    ) = (
        lax.all_gather(ln1_gain, "mp", axis=0, tiled=True),
        lax.all_gather(ln1_bias, "mp", axis=0, tiled=True),
        lax.all_gather(ln2_gain, "mp", axis=0, tiled=True),
        lax.all_gather(ln2_bias, "mp", axis=0, tiled=True),
        lax.all_gather(b_out, "mp", axis=0, tiled=True),
        lax.all_gather(b_down, "mp", axis=0, tiled=True),
        lax.all_gather(b_up, "mp", axis=0, tiled=True),
        lax.all_gather(w_out, "mp", axis=0, tiled=True),
        lax.all_gather(w_up, "mp", axis=1, tiled=True),
        lax.all_gather(w_down, "mp", axis=0, tiled=True),
    )
    gain_one = gain_one.astype(jnp.float32)
    shift_one = shift_one.astype(jnp.float32)
    gain_two = gain_two.astype(jnp.float32)
    shift_two = shift_two.astype(jnp.float32)
    tokens_wide = tokens.astype(jnp.float32)
    normed = layer_norm(tokens_wide, gain_one, shift_one).astype(jnp.bfloat16)
    query = (plain_dot(normed, w_qkv[0]) + b_qv[0].astype(jnp.float32)).astype(jnp.bfloat16)
    key_rows = plain_dot(normed, w_qkv[1]).astype(jnp.bfloat16)
    value_rows = (plain_dot(normed, w_qkv[2]) + b_qv[1].astype(jnp.float32)).astype(jnp.bfloat16)
    shaped = (sequences, LEN, heads_here, HD)
    query_seq = query.reshape(shaped)
    key_seq = key_rows.reshape(shaped)
    value_seq = value_rows.reshape(shaped)
    segment_seq = segment.reshape(sequences, LEN)
    attended, log_total = lax.map(attend_forward, (query_seq, key_seq, value_seq, segment_seq))
    attended = attended.reshape(group_rows, heads_here * HD)
    my_rows = lax.dynamic_slice_in_dim(tokens_wide, my_index * row_count, row_count, 0)
    attended_rows = lax.all_to_all(attended, "mp", split_axis=0, concat_axis=1, tiled=True)
    projected = plain_dot(attended_rows, full_out)
    hidden = my_rows + projected + bias_out.astype(jnp.float32)
    normed_two = layer_norm(hidden, gain_two, shift_two).astype(jnp.bfloat16)
    cot_wide = cotangent.astype(jnp.float32)
    up_proj = plain_dot(normed_two, full_up) + bias_up.astype(jnp.float32)
    active = gelu_exact(up_proj).astype(jnp.bfloat16)
    output = hidden + plain_dot(active, full_down) + bias_down.astype(jnp.float32)
    grad_up = gelu_back(up_proj, against(cotangent, full_down)).astype(jnp.bfloat16)
    grad_down = over_rows(active, cotangent)
    grad_upw = over_rows(normed_two, grad_up)
    grad_bias_up = jnp.sum(grad_up.astype(jnp.float32), axis=0)
    grad_normed_two = against(grad_up, full_up)
    grad_bias_down = jnp.sum(cot_wide, axis=0)
    grad_hidden_norm, grad_gain_two, grad_shift_two = norm_back(
        hidden, gain_two, shift_two, grad_normed_two
    )
    grad_hidden = cot_wide + grad_hidden_norm
    grad_bias_out = jnp.sum(grad_hidden, axis=0)
    grad_proj = grad_hidden.astype(jnp.bfloat16)
    grad_outw = over_rows(attended_rows, grad_proj)
    grad_attended = lax.all_to_all(
        against(grad_proj, full_out).astype(jnp.bfloat16),
        "mp",
        split_axis=1,
        concat_axis=0,
        tiled=True,
    )
    grad_query, grad_key, grad_value = lax.map(
        attend_backward,
        (query_seq, key_seq, value_seq, segment_seq, log_total, grad_attended.reshape(shaped)),
    )
    grad_query = grad_query.reshape(group_rows, heads_here * HD)
    grad_key = grad_key.reshape(group_rows, heads_here * HD)
    grad_value = grad_value.reshape(group_rows, heads_here * HD)
    grad_qkvw = jnp.stack(
        [over_rows(normed, grad_query), over_rows(normed, grad_key), over_rows(normed, grad_value)]
    )
    grad_bias_qv = jnp.stack(
        [
            jnp.sum(grad_query.astype(jnp.float32), axis=0),
            jnp.sum(grad_value.astype(jnp.float32), axis=0),
        ]
    )
    partial_normed = (
        against(grad_query, w_qkv[0]) + against(grad_key, w_qkv[1]) + against(grad_value, w_qkv[2])
    )
    grad_normed = lax.psum_scatter(
        partial_normed.astype(jnp.bfloat16), "mp", scatter_dimension=0, tiled=True
    ).astype(jnp.float32)
    grad_input_norm, grad_gain_one, grad_shift_one = norm_back(
        my_rows, gain_one, shift_one, grad_normed
    )
    grad_input = grad_hidden + grad_input_norm
    (
        share_gain_one,
        share_shift_one,
        share_gain_two,
        share_shift_two,
        share_bias_out,
        share_bias_down,
        share_bias_up,
        share_outw,
        share_upw,
        share_down,
    ) = (
        lax.psum_scatter(
            grad_gain_one.astype(jnp.bfloat16), "mp", scatter_dimension=0, tiled=True
        ).astype(jnp.float32),
        lax.psum_scatter(
            grad_shift_one.astype(jnp.bfloat16), "mp", scatter_dimension=0, tiled=True
        ).astype(jnp.float32),
        lax.psum_scatter(
            grad_gain_two.astype(jnp.bfloat16), "mp", scatter_dimension=0, tiled=True
        ).astype(jnp.float32),
        lax.psum_scatter(
            grad_shift_two.astype(jnp.bfloat16), "mp", scatter_dimension=0, tiled=True
        ).astype(jnp.float32),
        lax.psum_scatter(
            grad_bias_out.astype(jnp.bfloat16), "mp", scatter_dimension=0, tiled=True
        ).astype(jnp.float32),
        lax.psum_scatter(
            grad_bias_down.astype(jnp.bfloat16), "mp", scatter_dimension=0, tiled=True
        ).astype(jnp.float32),
        lax.psum_scatter(
            grad_bias_up.astype(jnp.bfloat16), "mp", scatter_dimension=0, tiled=True
        ).astype(jnp.float32),
        lax.psum_scatter(
            grad_outw.astype(jnp.bfloat16), "mp", scatter_dimension=0, tiled=True
        ).astype(jnp.float32),
        lax.psum_scatter(
            grad_upw.astype(jnp.bfloat16), "mp", scatter_dimension=1, tiled=True
        ).astype(jnp.float32),
        lax.psum_scatter(
            grad_down.astype(jnp.bfloat16), "mp", scatter_dimension=0, tiled=True
        ).astype(jnp.float32),
    )
    summed = lax.psum(
        (
            share_gain_one,
            share_shift_one,
            grad_qkvw,
            grad_bias_qv,
            share_outw,
            share_bias_out,
            share_gain_two,
            share_shift_two,
            share_upw,
            share_bias_up,
            share_down,
            share_bias_down,
        ),
        "dp",
    )
    return (
        output.astype(jnp.bfloat16),
        grad_input,
        summed[0],
        summed[1],
        summed[2],
        summed[3],
        summed[4],
        summed[5],
        summed[6],
        summed[7],
        summed[8],
        summed[9],
        summed[10],
        summed[11],
    )


def solution(mesh):
    placed = (
        P("dp", None),
        P("dp"),
        P("mp"),
        P("mp"),
        P(None, None, "mp"),
        P(None, "mp"),
        P("mp", None),
        P("mp"),
        P("mp"),
        P("mp"),
        P(None, "mp"),
        P("mp"),
        P("mp", None),
        P("mp"),
        P(("dp", "mp"), None),
    )
    return jax.shard_map(
        per_device,
        mesh=mesh,
        in_specs=placed,
        out_specs=(
            P(("dp", "mp"), None),
            P(("dp", "mp"), None),
            P("mp"),
            P("mp"),
            P(None, None, "mp"),
            P(None, "mp"),
            P("mp", None),
            P("mp"),
            P("mp"),
            P("mp"),
            P(None, "mp"),
            P("mp"),
            P("mp", None),
            P("mp"),
        ),
        check_vma=False,
    )
```

profile of v0, /device:TPU:0, one launch (start us, length us, event | category | flops | bytes accessed | tf_op | source)
XLA Modules:
  0.0 748.0 jit_solution(18345992957422097749)
XLA Ops:
  14.9 13.4 %all-reduce.15 = (bf16[768]{0:T(1024)(128)(2,1)S(1)}, bf16[768]{0:T(1024)(128)(2,1)S(1)}, bf16[768]{0:T(1024)(128)(2,1)S(1)}, bf16[768]{0:T(1024)(128)(2,1)S(1)}, bf16[768]{0:T(1024)(128)(2,1)S(1)}) all-reduce(bf16[768]{0:T(1024)(128)(2,1)S(1)} %dynamic-update-slice.1, ...), channel_id=1, replica_groups=mesh['dp'=8,'mp'=4] {'mp'}, use_global_device_ids=true, to_apply=%add.1 | all-reduce | flops 3840 | bytes 15360
  28.3 8.6 %copy.80 = bf16[4096,768]{0,1:T(8,128)(2,1)} copy(bf16[4096,768]{1,0:T(8,128)(2,1)} %param.19) | data formatting | bytes 12582912 | tf_op args[0]
  36.9 4.7 convert_reduce_fusion
  58.4 40.7 %while.26 = (s32[]{:T(128)}, bf16[8,512,3,64]{1,3,2,0:T(8,128)(2,1)}, f32[8,3,512]{2,1,0:T(4,128)}, bf16[8,512,3,64]{1,3,2,0:T(8,128)(2,1)}, s32[8,512]{1,0:T(8,...) while((s32[]{:T(128)}, ...), condition=%wide.region_5.6_spmd, body=%wide.region_2.5_spmd.sunk | while | flops 211909632 | bytes 11333209 | solution.py:166
  99.2 4.6 copy.84
  103.7 3.7 all_to_all.26
  110.5 3.6 all-to-all-start
  114.9 9.2 %convert_element_type.163 = f32[4096,768]{0,1:T(8,128)} convert(bf16[4096,768]{0,1:T(8,128)(2,1)} %copy.80) | non-fusion elementwise | flops 3145728 | bytes 18874368 | tf_op jit(solution)/shard_map/convert_element_type | solution.py:156
  124.1 16.9 %all-gather = bf16[4,1,768]{2,1,0:T(2,128)(2,1)S(1)} all-gather(bf16[1,1,768]{2,1,0:T(2,128)(2,1)S(1)} %reshape.310), channel_id=1, replica_groups=mesh['dp'=8,'mp'=4] {'mp'}, dimensions={0}, use_global_device_ids=true | all-gather | bytes 7680 | tf_op jit(solution)/shard_map/all_gather | solution.py:147
  143.8 4.3 fusion.91
  148.5 37.7 %multiply_convert_fusion.1 = (bf16[1024,3072]{1,0:T(8,128)(2,1)}, f32[1024,3072]{1,0:T(8,128)}, f32[1024,3072]{1,0:T(8,128)}) fusion(f32[3072]{0:T(1024)S(1)} %bitcast.224, bf16[768,3072]{1,0:T(8,128)(2,1)} %all-gather.7.cloned.1.call-done, f32[1024,768]{0,1:T(8,128)S(1)} %get-tuple-element.289, f32[768]{0:T(1024)S(1)} %convert_element_type.172, ...), kind=kOutput, calls=%fused_computation.70 | convolution fusion | flops 5043388416 | bytes 39348224 | tf_op jit(solution)/shard_map/dot_general | solution.py:31
  186.2 18.7 %fusion.93 = (bf16[3072]{0:T(1024)(128)(2,1)S(1)}, bf16[1024,3072]{1,0:T(8,128)(2,1)}) fusion(f32[1024,3072]{1,0:T(8,128)} %get-tuple-element.275, bf16[1024,768]{1,0:T(8,128)(2,1)} %param.33, bf16[3072,768]{1,0:T(8,128)(2,1)} %all-gather.9.cloned.1.call-done, f32[1024,3072]{1,0:T(8,128)} %get-tuple-element.290, f32[3072]{0:T(1024)S(1)} %bitcast.225), kind=kOutput, calls=%fused_computation.165 | convolution fusion | flops 4882166784 | bytes 37767168 | tf_op jit(solution)/shard_map/dot_general | solution.py:41
  204.9 9.8 %fusion.92 = (bf16[768]{0:T(1024)(128)(2,1)S(1)}, f32[1024,768]{1,0:T(8,128)}) fusion(bf16[1024,3072]{1,0:T(8,128)(2,1)} %get-tuple-element.294, bf16[768,3072]{1,0:T(8,128)(2,1)} %all-gather.7.cloned.1.call-done), kind=kOutput, calls=%fused_computation.164 | convolution fusion | flops 4832623616 | bytes 14157312 | tf_op jit(solution)/shard_map/dot_general | solution.py:41
  214.7 3.6 copy.88
  227.4 9.9 %convolution_convert_fusion.1 = bf16[768,3072]{1,0:T(8,128)(2,1)} fusion(bf16[1024,3072]{1,0:T(8,128)(2,1)} %get-tuple-element.294, f32[1024,768]{0,1:T(8,128)S(1)} %get-tuple-element.289, f32[768]{0:T(1024)S(1)} %convert_element_type.172, f32[768]{0:T(1024)S(1)} %convert_element_type.171, f32[1024]{0:T(1024)S(1)} %fusion.85, ...), kind=kOutput, calls=%fused_computation.88 | convolution fusion | flops 4838129664 | bytes 14170112 | tf_op jit(solution)/shard_map/dot_general | solution.py:35
  237.3 4.3 convolution_convert_fusion.3
  241.6 4.4 all-to-all-start.1
  246.1 9.1 %convolution_convert_fusion = bf16[3072,768]{1,0:T(8,128)(2,1)} fusion(bf16[1024,3072]{1,0:T(8,128)(2,1)} %get-tuple-element.274, bf16[1024,768]{1,0:T(8,128)(2,1)} %param.33), kind=kOutput, calls=%fused_computation.87 | convolution fusion | flops 4834197504 | bytes 12582912 | tf_op jit(solution)/shard_map/dot_general | solution.py:35
  255.3 14.3 %all-to-all-done.1 = bf16[1024,4,192]{0,2,1:T(8,128)(2,1)} async-done(((bf16[1024,4,192]{0,2,1:T(8,128)(2,1)}), bf16[1024,4,192]{0,2,1:T(8,128)(2,1)}, u32[]{:S(2)}, u32[]{:S(2)}) %all-to-all-start.1) | async-done | bytes 1572896 | tf_op jit(solution)/shard_map/all_to_all | solution.py:190
  269.6 3.9 copy.89
  284.1 102.6 %while.27 = (s32[]{:T(128)}, bf16[8,512,3,64]{1,3,2,0:T(8,128)(2,1)}, bf16[8,512,3,64]{1,3,2,0:T(8,128)(2,1)}, bf16[8,512,3,64]{1,3,2,0:T(8,128)(2,1)}, bf16[8,5...) while((s32[]{:T(128)}, ...), condition=%wide.region_12.13_spmd, body=%wide.region_10.12_spmd.sunk | while | flops 511933440 | bytes 26126452 | solution.py:197
  393.4 6.4 fusion.71
  399.8 6.3 fusion.74
  406.1 12.1 %add_convert_fusion = bf16[4096,768]{0,1:T(8,128)(2,1)} fusion(f32[4096,768]{0,1:T(8,128)} %fusion.74, f32[4096,768]{0,1:T(8,128)} %fusion.71, bf16[4096,192]{0,1:T(8,128)(2,1)S(1)} %bitcast.206, bf16[3,768,192]{1,2,0:T(8,128)(2,1)S(1)} %copy-done.24), kind=kOutput, calls=%fused_computation.68 | convolution fusion | flops 1217396736 | bytes 33325056 | tf_op jit(solution)/shard_map/dot_general | solution.py:41
  427.1 6.8 convolution_bitcast_fusion
  434.0 5.2 convolution_bitcast_fusion.1
  442.9 33.4 %reduce-scatter.5.cloned.1.call-done = bf16[1024,768]{0,1:T(8,128)(2,1)} async-done(((bf16[4096,768]{0,1:T(8,128)(2,1)}), bf16[1024,768]{0,1:T(8,128)(2,1)}) %reduce-scatter.5.cloned.1.call-update) | async-done | bytes 1572880 | tf_op jit(solution)/shard_map/reduce_scatter | solution.py:216
  479.6 3.6 fusion.67
  483.2 5.3 add_add_fusion.2
  490.2 11.2 %all-reduce.14 = (bf16[768]{0:T(1024)(128)(2,1)S(1)}, bf16[768]{0:T(1024)(128)(2,1)S(1)}, bf16[768]{0:T(1024)(128)(2,1)S(1)}, bf16[768]{0:T(1024)(128)(2,1)S(1)}...) all-reduce(bf16[768]{0:T(1024)(128)(2,1)S(1)} %dynamic-update-slice, ...), channel_id=1, replica_groups=mesh['dp'=8,'mp'=4] {'mp'}, use_global_device_ids=true, to_apply=%add.5 | all-reduce | flops 8448 | bytes 33792
  501.4 9.5 %add_convert_fusion.3 = bf16[1024,768]{0,1:T(8,128)(2,1)} fusion(f32[1024,768]{0,1:T(8,128)S(1)} %get-tuple-element.289, bf16[1024,3072]{1,0:T(8,128)(2,1)} %get-tuple-element.274, bf16[3072,768]{1,0:T(8,128)(2,1)} %all-gather.9.cloned.1.call-done, f32[768]{0:T(1024)S(1)} %convert_element_type.176), kind=kOutput, calls=%fused_computation.109 | convolution fusion | flops 4834197504 | bytes 15731712 | tf_op jit(solution)/shard_map/dot_general | solution.py:31
  516.4 221.8 %all-reduce.20 = (f32[192]{0:T(256)}, f32[192]{0:T(256)}, f32[2,192]{1,0:T(2,128)}, f32[192,768]{1,0:T(8,128)}, f32[192]{0:T(256)}, /*index=5*/f32[192]{0:T(256)...) all-reduce(f32[192]{0:T(256)S(1)} %get-tuple-element.302, ...), channel_id=1, replica_groups=mesh['dp'=8,'mp'=4] {'dp'}, use_global_device_ids=true, to_apply=%region_20.21 | all-reduce | flops 1329408 | bytes 7981056 | tf_op jit(solution)/shard_map/psum | solution.py:266
  (295 shorter events, 224.1 us)
Async XLA Ops:
  7.2 135.5 %all-gather.5.cloned.1.call-start = ((), (), s32[]{:S(2)}) async-start(), calls=%async_computation.6 | async-start | bytes 1474560 | tf_op jit(solution)/shard_map/all_gather | solution.py:148
  7.9 140.6 %all-gather.7.cloned.1.call-start = ((), (), s32[]{:S(2)}) async-start(), calls=%async_computation.7 | async-start | bytes 5898240 | tf_op jit(solution)/shard_map/all_gather | solution.py:149
  28.3 16.4 %copy-start.26 = (f32[768]{0:T(1024)}, f32[768]{0:T(1024)S(1)}, u32[]{:S(2)}) copy-start(f32[768]{0:T(1024)S(1)} %convert_element_type.164) | copy-start | bytes 9220
  36.9 6.0 copy-start
  44.7 3.5 copy-start.23
  48.2 5.1 copy-start.19
  99.2 8.3 %copy-start.9 = (bf16[8,512,3,64]{1,3,2,0:T(8,128)(2,1)}, bf16[8,512,3,64]{1,3,2,0:T(8,128)(2,1)S(1)}, u32[]{:S(2)}) copy-start(bf16[8,512,3,64]{1,3,2,0:T(8,128)(2,1)S(1)} %get-tuple-element.505) | copy-start | bytes 4718596
  99.2 8.3 %copy-start.10 = (bf16[8,512,3,64]{1,3,2,0:T(8,128)(2,1)}, bf16[8,512,3,64]{1,3,2,0:T(8,128)(2,1)S(1)}, u32[]{:S(2)}) copy-start(bf16[8,512,3,64]{1,3,2,0:T(8,128)(2,1)S(1)} %get-tuple-element.506) | copy-start | bytes 4718596
  99.2 8.3 %copy-start.28 = (s32[8,512]{1,0:T(8,128)}, s32[8,512]{1,0:T(8,128)S(1)}, u32[]{:S(2)}) copy-start(s32[8,512]{1,0:T(8,128)S(1)} %get-tuple-element.531) | copy-start | bytes 49156
  110.5 32.2 %all-to-all-start = ((bf16[4,1024,192]{1,2,0:T(8,128)(2,1)}), bf16[4,1024,192]{1,2,0:T(8,128)(2,1)S(1)}, u32[]{:S(2)}, u32[]{:S(2)}) async-start(bf16[4,1024,192]{1,2,0:T(8,128)(2,1)} %copy.85), calls=%async_computation | async-start | bytes 3145728 | tf_op jit(solution)/shard_map/all_to_all | solution.py:169
  114.1 72.2 %all-gather.9.cloned.1.call-start = ((), (), s32[]{:S(2)}) async-start(), calls=%async_computation.8 | async-start | bytes 5898240 | tf_op jit(solution)/shard_map/all_gather | solution.py:150
  114.8 9.3 %copy-start.31 = (bf16[768]{0:T(1024)(128)(2,1)S(1)}, bf16[768]{0:T(1024)(128)(2,1)}, u32[]{:S(2)}) copy-start(bf16[768]{0:T(1024)(128)(2,1)} %param.30) | copy-start | bytes 4612
  114.8 26.2 %copy-start.17 = (bf16[1024,768]{1,0:T(8,128)(2,1)S(1)}, bf16[1024,768]{1,0:T(8,128)(2,1)}, u32[]{:S(2)}) copy-start(bf16[1024,768]{1,0:T(8,128)(2,1)} %param.33) | copy-start | bytes 4718596
  114.8 328.0 %reduce-scatter.7.cloned.1.call-start = ((), (), s32[]{:S(2)}) async-start(), calls=%async_computation.11 | async-start | bytes 1474560 | tf_op jit(solution)/shard_map/reduce_scatter | solution.py:256
  227.4 215.5 %reduce-scatter.9.cloned.1.call-start = ((), (), s32[]{:S(2)}) async-start(), calls=%async_computation.12 | async-start | bytes 5898240 | tf_op jit(solution)/shard_map/reduce_scatter | solution.py:259
  241.6 27.9 %all-to-all-start.1 = ((bf16[1024,4,192]{0,2,1:T(8,128)(2,1)}), bf16[1024,4,192]{0,2,1:T(8,128)(2,1)}, u32[]{:S(2)}, u32[]{:S(2)}) async-start(bf16[1024,4,192]{0,2,1:T(8,128)(2,1)} %bitcast.218), calls=%async_computation.1 | async-start | bytes 3145728 | tf_op jit(solution)/shard_map/all_to_all | solution.py:190
  246.1 196.8 %reduce-scatter.11.cloned.1.call-start = ((), (), s32[]{:S(2)}) async-start(), calls=%async_computation.13 | async-start | bytes 5898240 | tf_op jit(solution)/shard_map/reduce_scatter | solution.py:262
  255.3 221.0 %reduce-scatter.5.cloned.1.call-start = ((), (), s32[]{:S(2)}) async-start(), calls=%async_computation.9 | async-start | bytes 7864320 | tf_op jit(solution)/shard_map/reduce_scatter | solution.py:216
  386.7 3.1 copy-start.18
  389.8 16.3 %copy-start.16 = (bf16[24,8,8,512]{3,1,2,0:T(8,128)(2,1)}, bf16[24,8,8,512]{3,1,2,0:T(8,128)(2,1)S(1)}, u32[]{:S(2)}) copy-start(bf16[24,8,8,512]{3,1,2,0:T(8,128)(2,1)S(1)} %copy.116) | copy-start | bytes 4718596
  393.3 6.5 copy-start.14
  418.3 3.1 copy-start.32
  418.3 319.9 %all-reduce.19.cloned.1.call-start = ((), (), s32[]{:S(2)}) async-start(), calls=%async_computation.10 | async-start | bytes 3538944 | tf_op jit(solution)/shard_map/psum | solution.py:266
  422.0 3.0 copy-start.8
  427.1 6.8 copy-start.13
  427.1 12.0 %slice-start = ((s8[6291456]{0:T(1024)(128)(4,1)}), s8[4194304]{0:T(1024)(128)(4,1)S(1)}, s32[]{:S(2)}) async-start(s8[6291456]{0:T(1024)(128)(4,1)} %bitcast.214), calls=%async_computation.14 | async-start | bytes 8388608
  434.0 5.2 copy-start.15
  434.0 5.2 slice-start.1
  441.4 34.9 %copy-start.27 = (f32[768]{0:T(1024)S(1)}, f32[768]{0:T(1024)}, u32[]{:S(2)}) copy-start(f32[768]{0:T(1024)} %copy-done.26) | copy-start | bytes 9220
  476.3 3.3 copy-start.4
  479.5 3.7 copy-start.3
  479.5 3.7 copy-start.6
  (13 other events, 24.4 us)
Sparse Core Ops, SparseCore 0:
  9.5 20.3 all-gather.4
  31.5 37.4 all-gather.6
  116.4 44.5 all-gather.8
  227.5 29.6 reduce-scatter.6
  259.6 47.4 reduce-scatter.8
  309.5 47.9 reduce-scatter.10
  418.4 57.8 reduce-scatter.4
  480.4 120.0 all-reduce.18
where the time goes:
time: 760 us; the launch traced here: 748 us
  blocking collectives  263 us (35%)
  matrix products  259 us (34%)
  local copies, waits for them, and re-layouts  77.2 us (10%)
  other arithmetic  73.1 us (10%)
  waiting for transfers between devices  49.9 us (7%)
  between operations  16.9 us (2%)
  starting transfers between devices  8.29 us (1%)
    psum x1, blocking collectives, per_device(): lax.psum((share_gain_one, share_shift_one, grad_qkvw, grad_bias_qv, share...  222 us
    dot_general x6, matrix products, against(): lax.dot_general(left, right, (((1,), (1,)), ((), ())), preferred_element_...  57.6 us
    dot_general x6, matrix products, plain_dot(): return jnp.dot(left, right, preferred_element_type=jnp.float32)  55.7 us
    dot_general x6, matrix products, over_rows(): lax.dot_general(left, right, (((0,), (0,)), ((), ())), preferred_element_...  35.7 us
    unnamed x95, local copies, waits for them, and re-layouts  33.9 us
    reduce_scatter x1, waiting for transfers between devices, per_device(): lax.psum_scatter(partial_normed.astype(jnp.bfloat16), 'mp', scatter_dimen...  33.4 us
    unnamed x2, blocking collectives  24.6 us
    dot_general x16, matrix products, head_scores(): jnp.einsum('qhd,khd->hqk', query_heads, key_heads, preferred_element_type...  23.6 us
  transfers between devices with their start and end apart: 10, of which 2 were waited for; matrix products, arithmetic and copies ran while one was open for 48% of the time, Pallas kernels for 0%

commit v1 on v0

--- a/solution.py
+++ b/solution.py
@@ -1,3 +1,4 @@
+import functools
 import jax
 import jax.numpy as jnp
 from jax import lax
@@ -5,6 +6,17 @@
 
 HD = 64
 LEN = 512
+
+
+def store_layers_all(u_in, row_axis):
+    then = jnp.split(u_in, lax.axis_size(row_axis), axis=1)
+    vec_out = jnp.stack(then)
+    plain = lax.all_to_all(vec_out, row_axis, 0, 0)
+    tile_out = jnp.concatenate(plain, axis=0)
+    return tile_out
+
+
+_extend_sources_all = functools.partial(store_layers_all, row_axis="mp")
 
 
 def layer_norm(values, norm_gain, norm_shift):
@@ -187,13 +199,7 @@
     grad_bias_out = jnp.sum(grad_hidden, axis=0)
     grad_proj = grad_hidden.astype(jnp.bfloat16)
     grad_outw = over_rows(attended_rows, grad_proj)
-    grad_attended = lax.all_to_all(
-        against(grad_proj, full_out).astype(jnp.bfloat16),
-        "mp",
-        split_axis=1,
-        concat_axis=0,
-        tiled=True,
-    )
+    grad_attended = _extend_sources_all(against(grad_proj, full_out).astype(jnp.bfloat16))
     grad_query, grad_key, grad_value = lax.map(
         attend_backward,
         (query_seq, key_seq, value_seq, segment_seq, log_total, grad_attended.reshape(shaped)),

time: 760 us -> 760 us (level)
  no operation moved by 1% of the time
where the time goes in v1:
time: 760 us; the launch traced here: 748 us
  blocking collectives  263 us (35%)
  matrix products  257 us (34%)
  local copies, waits for them, and re-layouts  77.6 us (10%)
  other arithmetic  74.8 us (10%)
  waiting for transfers between devices  49.4 us (6%)
  between operations  16.9 us (2%)
  starting transfers between devices  8.25 us (1%)
    psum x1, blocking collectives, per_device(): lax.psum((share_gain_one, share_shift_one, grad_qkvw, grad_bias_qv, share...  222 us
    dot_general x6, matrix products, against(): lax.dot_general(left, right, (((1,), (1,)), ((), ())), preferred_element_...  56.5 us
    dot_general x6, matrix products, plain_dot(): return jnp.dot(left, right, preferred_element_type=jnp.float32)  55.7 us
    dot_general x6, matrix products, over_rows(): lax.dot_general(left, right, (((0,), (0,)), ((), ())), preferred_element_...  35.5 us
    unnamed x95, local copies, waits for them, and re-layouts  33.9 us
    reduce_scatter x1, waiting for transfers between devices, per_device(): lax.psum_scatter(partial_normed.astype(jnp.bfloat16), 'mp', scatter_dimen...  33.2 us
    unnamed x2, blocking collectives  24.6 us
    dot_general x16, matrix products, head_scores(): jnp.einsum('qhd,khd->hqk', query_heads, key_heads, preferred_element_type...  23.6 us
  transfers between devices with their start and end apart: 10, of which 2 were waited for; matrix products, arithmetic and copies ran while one was open for 48% of the time, Pallas kernels for 0%

profile of v1, /device:TPU:0, one launch (start us, length us, event | category | flops | bytes accessed | tf_op | source)
XLA Modules:
  0.0 747.9 jit_solution(5415918857712550685)
XLA Ops:
  14.9 13.4 %all-reduce.15 = (bf16[768]{0:T(1024)(128)(2,1)S(1)}, bf16[768]{0:T(1024)(128)(2,1)S(1)}, bf16[768]{0:T(1024)(128)(2,1)S(1)}, bf16[768]{0:T(1024)(128)(2,1)S(1)}, bf16[768]{0:T(1024)(128)(2,1)S(1)}) all-reduce(bf16[768]{0:T(1024)(128)(2,1)S(1)} %dynamic-update-slice.1, ...), channel_id=1, replica_groups=mesh['dp'=8,'mp'=4] {'mp'}, use_global_device_ids=true, to_apply=%add.1 | all-reduce | flops 3840 | bytes 15360
  28.3 8.6 %copy.80 = bf16[4096,768]{0,1:T(8,128)(2,1)} copy(bf16[4096,768]{1,0:T(8,128)(2,1)} %param.19) | data formatting | bytes 12582912 | tf_op args[0]
  36.9 4.7 convert_reduce_fusion
  58.4 40.7 %while.26 = (s32[]{:T(128)}, bf16[8,512,3,64]{1,3,2,0:T(8,128)(2,1)}, f32[8,3,512]{2,1,0:T(4,128)}, bf16[8,512,3,64]{1,3,2,0:T(8,128)(2,1)}, s32[8,512]{1,0:T(8,...) while((s32[]{:T(128)}, ...), condition=%wide.region_5.6_spmd, body=%wide.region_2.5_spmd.sunk | while | flops 211909632 | bytes 11333209 | solution.py:178
  99.2 4.6 copy.84
  103.7 3.7 all_to_all.17
  110.5 3.6 all-to-all-start
  114.9 9.2 %convert_element_type.163 = f32[4096,768]{0,1:T(8,128)} convert(bf16[4096,768]{0,1:T(8,128)(2,1)} %copy.80) | non-fusion elementwise | flops 3145728 | bytes 18874368 | tf_op jit(solution)/shard_map/convert_element_type | solution.py:168
  124.1 16.9 %all-gather = bf16[4,1,768]{2,1,0:T(2,128)(2,1)S(1)} all-gather(bf16[1,1,768]{2,1,0:T(2,128)(2,1)S(1)} %reshape.302), channel_id=1, replica_groups=mesh['dp'=8,'mp'=4] {'mp'}, dimensions={0}, use_global_device_ids=true | all-gather | bytes 7680 | tf_op jit(solution)/shard_map/all_gather | solution.py:159
  143.8 4.3 fusion.91
  148.5 37.7 %multiply_convert_fusion.1 = (bf16[1024,3072]{1,0:T(8,128)(2,1)}, f32[1024,3072]{1,0:T(8,128)}, f32[1024,3072]{1,0:T(8,128)}) fusion(f32[3072]{0:T(1024)S(1)} %bitcast.229, bf16[768,3072]{1,0:T(8,128)(2,1)} %all-gather.7.cloned.1.call-done, f32[1024,768]{0,1:T(8,128)S(1)} %get-tuple-element.293, f32[768]{0:T(1024)S(1)} %convert_element_type.172, ...), kind=kOutput, calls=%fused_computation.70 | convolution fusion | flops 5043388416 | bytes 39348224 | tf_op jit(solution)/shard_map/dot_general | solution.py:43
  186.2 18.7 %fusion.93 = (bf16[3072]{0:T(1024)(128)(2,1)S(1)}, bf16[1024,3072]{1,0:T(8,128)(2,1)}) fusion(f32[1024,3072]{1,0:T(8,128)} %get-tuple-element.275, bf16[1024,768]{1,0:T(8,128)(2,1)} %param.33, bf16[3072,768]{1,0:T(8,128)(2,1)} %all-gather.9.cloned.1.call-done, f32[1024,3072]{1,0:T(8,128)} %get-tuple-element.294, f32[3072]{0:T(1024)S(1)} %bitcast.230), kind=kOutput, calls=%fused_computation.170 | convolution fusion | flops 4882166784 | bytes 37767168 | tf_op jit(solution)/shard_map/dot_general | solution.py:53
  204.9 9.8 %fusion.92 = (bf16[768]{0:T(1024)(128)(2,1)S(1)}, f32[1024,768]{1,0:T(8,128)}) fusion(bf16[1024,3072]{1,0:T(8,128)(2,1)} %get-tuple-element.298, bf16[768,3072]{1,0:T(8,128)(2,1)} %all-gather.7.cloned.1.call-done), kind=kOutput, calls=%fused_computation.169 | convolution fusion | flops 4832623616 | bytes 14157312 | tf_op jit(solution)/shard_map/dot_general | solution.py:53
  214.7 3.6 copy.88
  227.4 9.9 %convolution_convert_fusion.1 = bf16[768,3072]{1,0:T(8,128)(2,1)} fusion(bf16[1024,3072]{1,0:T(8,128)(2,1)} %get-tuple-element.298, f32[1024,768]{0,1:T(8,128)S(1)} %get-tuple-element.293, f32[768]{0:T(1024)S(1)} %convert_element_type.172, f32[768]{0:T(1024)S(1)} %convert_element_type.171, f32[1024]{0:T(1024)S(1)} %fusion.85, ...), kind=kOutput, calls=%fused_computation.88 | convolution fusion | flops 4838129664 | bytes 14170112 | tf_op jit(solution)/shard_map/dot_general | solution.py:47
  242.0 4.4 all-to-all-start.1
  246.4 9.1 %convolution_convert_fusion = bf16[3072,768]{1,0:T(8,128)(2,1)} fusion(bf16[1024,3072]{1,0:T(8,128)(2,1)} %get-tuple-element.274, bf16[1024,768]{1,0:T(8,128)(2,1)} %param.33), kind=kOutput, calls=%fused_computation.87 | convolution fusion | flops 4834197504 | bytes 12582912 | tf_op jit(solution)/shard_map/dot_general | solution.py:47
  255.6 14.0 %all-to-all-done.1 = bf16[4,1024,192]{1,2,0:T(8,128)(2,1)} async-done(((bf16[4,1024,192]{1,2,0:T(8,128)(2,1)}), bf16[4,1024,192]{1,2,0:T(8,128)(2,1)}, u32[]{:S(2)}, u32[]{:S(2)}) %all-to-all-start.1) | async-done | bytes 1572896 | tf_op jit(solution)/shard_map/all_to_all | solution.py:14
  269.6 3.9 copy.89
  273.4 3.5 reshape_reshape.3
  284.3 102.6 %while.27 = (s32[]{:T(128)}, bf16[8,512,3,64]{1,3,2,0:T(8,128)(2,1)}, bf16[8,512,3,64]{1,3,2,0:T(8,128)(2,1)}, bf16[8,512,3,64]{1,3,2,0:T(8,128)(2,1)}, bf16[8,5...) while((s32[]{:T(128)}, ...), condition=%wide.region_12.13_spmd, body=%wide.region_10.12_spmd.sunk | while | flops 511933440 | bytes 26126452 | solution.py:203
  393.6 6.4 fusion.71
  400.0 6.3 fusion.74
  406.3 12.1 %add_convert_fusion = bf16[4096,768]{0,1:T(8,128)(2,1)} fusion(f32[4096,768]{0,1:T(8,128)} %fusion.74, f32[4096,768]{0,1:T(8,128)} %fusion.71, bf16[4096,192]{0,1:T(8,128)(2,1)S(1)} %bitcast.212, bf16[3,768,192]{1,2,0:T(8,128)(2,1)S(1)} %copy-done.24), kind=kOutput, calls=%fused_computation.68 | convolution fusion | flops 1217396736 | bytes 33325056 | tf_op jit(solution)/shard_map/dot_general | solution.py:53
  427.6 6.6 convolution_bitcast_fusion
  434.2 5.2 convolution_bitcast_fusion.1
  443.1 33.2 %reduce-scatter.5.cloned.1.call-done = bf16[1024,768]{0,1:T(8,128)(2,1)} async-done(((bf16[4096,768]{0,1:T(8,128)(2,1)}), bf16[1024,768]{0,1:T(8,128)(2,1)}) %reduce-scatter.5.cloned.1.call-update) | async-done | bytes 1572880 | tf_op jit(solution)/shard_map/reduce_scatter | solution.py:222
  479.6 3.6 fusion.67
  483.2 5.3 add_add_fusion.2
  490.2 11.2 %all-reduce.14 = (bf16[768]{0:T(1024)(128)(2,1)S(1)}, bf16[768]{0:T(1024)(128)(2,1)S(1)}, bf16[768]{0:T(1024)(128)(2,1)S(1)}, bf16[768]{0:T(1024)(128)(2,1)S(1)}...) all-reduce(bf16[768]{0:T(1024)(128)(2,1)S(1)} %dynamic-update-slice, ...), channel_id=1, replica_groups=mesh['dp'=8,'mp'=4] {'mp'}, use_global_device_ids=true, to_apply=%add.5 | all-reduce | flops 8448 | bytes 33792
  501.4 9.5 %add_convert_fusion.3 = bf16[1024,768]{0,1:T(8,128)(2,1)} fusion(f32[1024,768]{0,1:T(8,128)S(1)} %get-tuple-element.293, bf16[1024,3072]{1,0:T(8,128)(2,1)} %get-tuple-element.274, bf16[3072,768]{1,0:T(8,128)(2,1)} %all-gather.9.cloned.1.call-done, f32[768]{0:T(1024)S(1)} %convert_element_type.176), kind=kOutput, calls=%fused_computation.109 | convolution fusion | flops 4834197504 | bytes 15731712 | tf_op jit(solution)/shard_map/dot_general | solution.py:43
  516.4 221.7 %all-reduce.20 = (f32[192]{0:T(256)}, f32[192]{0:T(256)}, f32[2,192]{1,0:T(2,128)}, f32[192,768]{1,0:T(8,128)}, f32[192]{0:T(256)}, /*index=5*/f32[192]{0:T(256)...) all-reduce(f32[192]{0:T(256)S(1)} %get-tuple-element.306, ...), channel_id=1, replica_groups=mesh['dp'=8,'mp'=4] {'dp'}, use_global_device_ids=true, to_apply=%region_20.21 | all-reduce | flops 1329408 | bytes 7981056 | tf_op jit(solution)/shard_map/psum | solution.py:272
  (297 shorter events, 225.7 us)
Async XLA Ops:
  7.2 135.5 %all-gather.5.cloned.1.call-start = ((), (), s32[]{:S(2)}) async-start(), calls=%async_computation.6 | async-start | bytes 1474560 | tf_op jit(solution)/shard_map/all_gather | solution.py:160
  7.9 140.6 %all-gather.7.cloned.1.call-start = ((), (), s32[]{:S(2)}) async-start(), calls=%async_computation.7 | async-start | bytes 5898240 | tf_op jit(solution)/shard_map/all_gather | solution.py:161
  28.3 16.4 %copy-start.26 = (f32[768]{0:T(1024)}, f32[768]{0:T(1024)S(1)}, u32[]{:S(2)}) copy-start(f32[768]{0:T(1024)S(1)} %convert_element_type.164) | copy-start | bytes 9220
  36.9 6.0 copy-start
  44.7 3.5 copy-start.23
  48.2 5.1 copy-start.19
  99.2 8.3 %copy-start.9 = (bf16[8,512,3,64]{1,3,2,0:T(8,128)(2,1)}, bf16[8,512,3,64]{1,3,2,0:T(8,128)(2,1)S(1)}, u32[]{:S(2)}) copy-start(bf16[8,512,3,64]{1,3,2,0:T(8,128)(2,1)S(1)} %get-tuple-element.509) | copy-start | bytes 4718596
  99.2 8.3 %copy-start.10 = (bf16[8,512,3,64]{1,3,2,0:T(8,128)(2,1)}, bf16[8,512,3,64]{1,3,2,0:T(8,128)(2,1)S(1)}, u32[]{:S(2)}) copy-start(bf16[8,512,3,64]{1,3,2,0:T(8,128)(2,1)S(1)} %get-tuple-element.510) | copy-start | bytes 4718596
  99.2 8.3 %copy-start.28 = (s32[8,512]{1,0:T(8,128)}, s32[8,512]{1,0:T(8,128)S(1)}, u32[]{:S(2)}) copy-start(s32[8,512]{1,0:T(8,128)S(1)} %get-tuple-element.535) | copy-start | bytes 49156
  110.5 32.2 %all-to-all-start = ((bf16[4,1024,192]{1,2,0:T(8,128)(2,1)}), bf16[4,1024,192]{1,2,0:T(8,128)(2,1)S(1)}, u32[]{:S(2)}, u32[]{:S(2)}) async-start(bf16[4,1024,192]{1,2,0:T(8,128)(2,1)} %copy.85), calls=%async_computation | async-start | bytes 3145728 | tf_op jit(solution)/shard_map/all_to_all | solution.py:181
  114.1 72.2 %all-gather.9.cloned.1.call-start = ((), (), s32[]{:S(2)}) async-start(), calls=%async_computation.8 | async-start | bytes 5898240 | tf_op jit(solution)/shard_map/all_gather | solution.py:162
  114.8 9.3 %copy-start.31 = (bf16[768]{0:T(1024)(128)(2,1)S(1)}, bf16[768]{0:T(1024)(128)(2,1)}, u32[]{:S(2)}) copy-start(bf16[768]{0:T(1024)(128)(2,1)} %param.30) | copy-start | bytes 4612
  114.8 26.2 %copy-start.17 = (bf16[1024,768]{1,0:T(8,128)(2,1)S(1)}, bf16[1024,768]{1,0:T(8,128)(2,1)}, u32[]{:S(2)}) copy-start(bf16[1024,768]{1,0:T(8,128)(2,1)} %param.33) | copy-start | bytes 4718596
  114.8 328.2 %reduce-scatter.7.cloned.1.call-start = ((), (), s32[]{:S(2)}) async-start(), calls=%async_computation.11 | async-start | bytes 1474560 | tf_op jit(solution)/shard_map/reduce_scatter | solution.py:262
  227.4 215.7 %reduce-scatter.9.cloned.1.call-start = ((), (), s32[]{:S(2)}) async-start(), calls=%async_computation.12 | async-start | bytes 5898240 | tf_op jit(solution)/shard_map/reduce_scatter | solution.py:265
  242.0 27.6 %all-to-all-start.1 = ((bf16[4,1024,192]{1,2,0:T(8,128)(2,1)}), bf16[4,1024,192]{1,2,0:T(8,128)(2,1)}, u32[]{:S(2)}, u32[]{:S(2)}) async-start(bf16[4,1024,192]{1,2,0:T(8,128)(2,1)} %pad_maximum_fusion.1), calls=%async_computation.1 | async-start | bytes 3145728 | tf_op jit(solution)/shard_map/all_to_all | solution.py:14
  246.3 196.7 %reduce-scatter.11.cloned.1.call-start = ((), (), s32[]{:S(2)}) async-start(), calls=%async_computation.13 | async-start | bytes 5898240 | tf_op jit(solution)/shard_map/reduce_scatter | solution.py:268
  255.6 220.7 %reduce-scatter.5.cloned.1.call-start = ((), (), s32[]{:S(2)}) async-start(), calls=%async_computation.9 | async-start | bytes 7864320 | tf_op jit(solution)/shard_map/reduce_scatter | solution.py:222
  386.9 3.1 copy-start.18
  390.0 16.3 %copy-start.16 = (bf16[24,8,8,512]{3,1,2,0:T(8,128)(2,1)}, bf16[24,8,8,512]{3,1,2,0:T(8,128)(2,1)S(1)}, u32[]{:S(2)}) copy-start(bf16[24,8,8,512]{3,1,2,0:T(8,128)(2,1)S(1)} %copy.116) | copy-start | bytes 4718596
  393.5 6.5 copy-start.14
  418.5 3.1 copy-start.32
  418.5 319.6 %all-reduce.19.cloned.1.call-start = ((), (), s32[]{:S(2)}) async-start(), calls=%async_computation.10 | async-start | bytes 3538944 | tf_op jit(solution)/shard_map/psum | solution.py:272
  422.2 3.3 copy-start.8
  427.6 6.6 copy-start.13
  427.6 11.8 %slice-start = ((s8[6291456]{0:T(1024)(128)(4,1)}), s8[4194304]{0:T(1024)(128)(4,1)S(1)}, s32[]{:S(2)}) async-start(s8[6291456]{0:T(1024)(128)(4,1)} %bitcast.220), calls=%async_computation.14 | async-start | bytes 8388608
  434.2 5.2 copy-start.15
  434.2 5.2 slice-start.1
  441.6 34.7 %copy-start.27 = (f32[768]{0:T(1024)S(1)}, f32[768]{0:T(1024)}, u32[]{:S(2)}) copy-start(f32[768]{0:T(1024)} %copy-done.26) | copy-start | bytes 9220
  476.3 3.3 copy-start.4
  479.5 3.7 copy-start.3
  479.5 3.7 copy-start.6
  (13 other events, 24.4 us)
Sparse Core Ops, SparseCore 0:
  9.5 20.3 all-gather.4
  31.5 37.4 all-gather.6
  116.4 44.5 all-gather.8
  227.5 29.3 reduce-scatter.6
  259.3 47.5 reduce-scatter.8
  309.2 47.9 reduce-scatter.10
  418.6 57.6 reduce-scatter.4
  480.4 120.1 all-reduce.18
